TPU v7x, 512 devices: a whole 4x8x8 slice. The times are simulated.
512 devices in a mesh: leaf: 32 (over z, x), slab: 16 (over y, core).
Axes of the slice: x: 4, y: 8, z: 8, core: 2. Of those that a mesh axis runs over, the one named last changes fastest.
Arguments:
- leaf_basis: bfloat16 [16, 256, 512, 128], P('slab', 'leaf'), may hold values from -0.25 to 0.25
- point_counts: int32 [16, 256], P('slab', 'leaf'), may hold values from 256 to 512, as said below
- leaf_transfer: float32 [16, 256, 128, 128], P('slab', 'leaf')
- node_transfer: float32 [16, 32, 128, 128], P('slab', 'leaf')
- group_transfer: float32 [16, 4, 128, 128], P('slab')
- positions: float32 [16, 256, 3, 512], P('slab', 'leaf'), may hold values from 0 to 2
- moments: float32 [16, 256, 512], P('slab', 'leaf'), may hold values from -6 to 6
- send_tiles: int32 [16, 128], P('slab', 'leaf'), may hold values from 0 to 7, as said below
- neighbours: int32 [16, 256, 4], P('slab', 'leaf'), may hold values from 0 to 11
Outputs:
- leaf_factors: float32 [16, 256, 128, 128], P('slab', 'leaf')
- node_factors: float32 [16, 32, 128, 128], P('slab', 'leaf')
- group_factors: float32 [16, 32, 128, 128], P('slab', 'leaf')
- root_factors: float32 [16, 32, 128, 128], P('slab', 'leaf')
- near_field: float32 [16, 256, 512], P('slab', 'leaf')
Inputs may be any that keep to these rules, and one draw needn't show every extreme that they name: `point_counts`: in each first-level node one leaf has all 512 slots live. `send_tiles`: within each node, the 2 lower-face and 2 upper-face entries name 4 different leaves of that node, numbered 0 to 7. `neighbours`: numbers below 8 are the node's own leaves; the next 2 are the faces received from the slab below, the last 2 those from the slab above.
All inputs are finite; a program needn't handle non-finite values.
Results may differ from a plain program's by a relative error of at most 0.0003.
Values sent between devices are 32-bit elements; how exact they have to be, the bound alone decides.
A program may use at most 64 MiB of HBM per device.

v0:
```python
import jax
import jax.numpy as jnp
from jax import lax
from jax.sharding import PartitionSpec as P

CHILDREN = 8


soften = 0.25
coupling = 0.03
highest = lax.Precision.HIGHEST


def from_partner(value, axis, apart):
    return lax.ppermute(value, axis, [(i, i ^ 1 << apart) for i in range(lax.axis_size(axis))])


def with_halo(cells, sides, width):
    for axis, dim in sides:
        count = lax.axis_size(axis)
        ends = count - 1
        head = lax.slice_in_dim(cells, 0, width, axis=dim)
        tail = lax.slice_in_dim(cells, cells.shape[dim] - width, cells.shape[dim], axis=dim)
        cells = jnp.concatenate(
            [
                lax.ppermute(tail, axis, [(i, (i + 1) % count) for i in range(ends)]),
                cells,
                lax.ppermute(head, axis, [((i + 1) % count, i) for i in range(ends)]),
            ],
            axis=dim,
        )
    return cells


def congruent(transfer, gram):
    inner = jnp.matmul(gram, transfer, precision=highest)
    return jnp.matmul(jnp.swapaxes(transfer, -1, -2), inner, precision=highest)


def near_tile(targets, sources):
    first_gap = targets[0][:, None, None] - sources[None, :, 0, :]
    second_gap = targets[1][:, None, None] - sources[None, :, 1, :]
    third_gap = targets[2][:, None, None] - sources[None, :, 2, :]
    radius = first_gap * first_gap + second_gap * second_gap + third_gap * third_gap + soften
    kernel = (radius - 3.0 * third_gap * third_gap) * radius ** (-2.5)
    return coupling * jnp.sum(kernel * sources[None, :, 3, :], axis=(1, 2))


def body(
    leaf_basis,
    point_counts,
    leaf_transfer,
    node_transfer,
    group_transfer,
    positions,
    moments,
    send_tiles,
    neighbours,
):
    basis = leaf_basis[0]
    counts = point_counts[0]
    leaves, points, width = basis.shape
    live = lax.broadcasted_iota(jnp.int32, (leaves, points), 1) < counts[:, None]
    masked = jnp.where(live[:, :, None], basis, jnp.zeros((), jnp.bfloat16))
    grams = lax.dot_general(
        masked, masked, (((1,), (1,)), ((0,), (0,))), preferred_element_type=jnp.float32
    )
    leaf_factors = jnp.linalg.cholesky(grams)
    node_gram = jnp.sum(congruent(leaf_transfer[0], grams), axis=0)
    node_factor = jnp.linalg.cholesky(node_gram)
    lifted = congruent(node_transfer[0, 0], node_gram)
    groups = group_transfer[0]
    position = lax.axis_index("leaf") // CHILDREN
    group_gram = lifted
    for bit in range(3):
        group_gram = group_gram + from_partner(group_gram, "leaf", bit)
    group_factor = jnp.linalg.cholesky(group_gram)
    own = lax.dynamic_index_in_dim(groups, position, 0, keepdims=False)
    root_gram = congruent(own, group_gram)
    for bit in range(3, lax.axis_size("leaf").bit_length() - 1):
        root_gram = root_gram + from_partner(root_gram, "leaf", bit)
    root_factor = jnp.linalg.cholesky(root_gram)
    charged = moments[0] * live.astype(jnp.float32)
    sources = jnp.concatenate([positions[0], charged[:, None, :]], axis=1)
    halo_width = send_tiles.shape[1] // 2
    faces = sources[send_tiles[0]].reshape(2, halo_width, 4, points)
    padded = with_halo(faces, (("slab", 0),), 1)
    extended = jnp.concatenate([sources, padded[0], padded[3]], axis=0)
    picked = extended[neighbours[0]]
    field = lax.map(lambda pair: near_tile(pair[0], pair[1]), (positions[0], picked))
    near = jnp.where(live, field, jnp.zeros((), jnp.float32))
    return (
        leaf_factors[None],
        node_factor[None, None],
        group_factor[None, None],
        root_factor[None, None],
        near[None],
    )


def solution(mesh):
    in_specs = (
        P("slab", "leaf", None, None),
        P("slab", "leaf"),
        P("slab", "leaf", None, None),
        P("slab", "leaf", None, None),
        P("slab", None, None, None),
        P("slab", "leaf", None, None),
        P("slab", "leaf", None),
        P("slab", "leaf"),
        P("slab", "leaf", None),
    )
    out_specs = (
        P("slab", "leaf", None, None),
        P("slab", "leaf", None, None),
        P("slab", "leaf", None, None),
        P("slab", "leaf", None, None),
        P("slab", "leaf", None),
    )
    return jax.shard_map(body, mesh=mesh, in_specs=in_specs, out_specs=out_specs, check_vma=False)
```

profile of v0, /device:TPU:1, one launch (start us, length us, event | category | flops | bytes accessed | tf_op | source)
XLA Modules:
  0.0 217.7 jit_solution(5963586791548624196)
XLA Ops:
  0.6 0.8 iota_compare_fusion.2
  1.4 3.4 %fusion.6 = f32[8,128,128]{2,1,0:T(8,128)S(1)} fusion(bf16[1,8,512,128]{3,2,1,0:T(8,128)(2,1)} %param.12, pred[8,512]{1,0:T(8,128)(4,1)S(1)} %iota_compare_fusion.2), kind=kOutput, calls=%fused_computation.23 | convolution fusion | flops 134742016 | bytes 1576960 | tf_op jit(solution)/shard_map/dot_general | solution.py:65
  4.9 1.0 fusion.10
  7.2 3.9 %collective-permute-start = (f32[128,128]{0,1:T(8,128)S(1)}, f32[128,128]{0,1:T(8,128)S(1)}, u32[]{:S(2)}, u32[]{:S(2)}) collective-permute-start(f32[128,128]{0,1:T(8,128)S(1)} %convolution_bitcast_fusion), channel_id=1, source_target_pairs={{0,16},{16,0},{32,48},{48,32},{64,80},{80,64},{96,112},{112,96},{1... | collective-permute-start | bytes 196616 | tf_op jit(solution)/shard_map/ppermute | solution.py:15
  12.0 4.0 %collective-permute-start.5 = (f32[1,2,4,512]{3,2,1,0:T(4,128)S(1)}, f32[1,2,4,512]{3,2,1,0:T(4,128)S(1)}, u32[]{:S(2)}, u32[]{:S(2)}) collective-permute-start(f32[1,2,4,512]{3,2,1,0:T(4,128)S(1)} %get-tuple-element.48), channel_id=1, source_target_pairs={{0,1},{1,2},{2,3},{3,4},{4,5},{5,6},{6,7},{7,8},{8,9},{9,10},{10,1... | collective-permute-start | bytes 49160 | tf_op jit(solution)/shard_map/ppermute | solution.py:26
  16.0 4.0 %collective-permute-start.6 = (f32[1,2,4,512]{3,2,1,0:T(4,128)S(1)}, f32[1,2,4,512]{3,2,1,0:T(4,128)S(1)}, u32[]{:S(2)}, u32[]{:S(2)}) collective-permute-start(f32[1,2,4,512]{3,2,1,0:T(4,128)S(1)} %get-tuple-element.49), channel_id=1, source_target_pairs={{1,0},{2,1},{3,2},{4,3},{5,4},{6,5},{7,6},{8,7},{9,8},{10,9},{11,1... | collective-permute-start | bytes 49160 | tf_op jit(solution)/shard_map/ppermute | solution.py:28
  20.4 11.7 %cholesky.98 = f32[128,128]{1,0:T(8,128)S(1)} custom-call(f32[128,128]{1,0:T(8,128)S(1)} %fusion.16), custom_call_target="Cholesky" | custom-call | tf_op jit(solution)/shard_map/jit(cholesky)/cholesky | solution.py:70
  32.8 1.3 select_bitcast_fusion.3
  34.3 93.8 %custom-call.6 = f32[8,128,128]{2,1,0:T(8,128)S(1)} custom-call(f32[8,128,128]{2,1,0:T(8,128)S(1)} %fusion.12), custom_call_target="Cholesky" | custom-call | tf_op jit(solution)/shard_map/jit(cholesky)/cholesky | solution.py:68
  128.2 0.9 select_bitcast_fusion
  129.2 0.7 gather_fusion.1
  130.0 2.5 %collective-permute-start.1 = (f32[128,128]{0,1:T(8,128)S(1)}, f32[128,128]{0,1:T(8,128)S(1)}, u32[]{:S(2)}, u32[]{:S(2)}) collective-permute-start(f32[128,128]{0,1:T(8,128)S(1)} %add.72), channel_id=1, source_target_pairs={{0,32},{16,48},{32,0},{48,16},{64,96},{80,112},{96,64},{112,80},{1... | collective-permute-start | bytes 196616 | tf_op jit(solution)/shard_map/ppermute | solution.py:15
  132.5 32.7 %while.11 = (s32[]{:T(128)}, f32[8,512]{1,0:T(8,128)S(1)}, f32[8,3,512]{2,1,0:T(4,128)S(1)}, f32[8,4,4,512]{3,2,1,0:T(4,128)S(1)}) while((s32[]{:T(128)}, f32[8,512]{1,0:T(8,128)S(1)}, f32[8,3,512]{2,1,0:T(4,128)S(1)}, f32[8,4,4,512]{3,2,1,0:T(4,128)S(1)}) %tuple.44), condition=%wide.region_6.8_spmd.clone, body=%wide.region_4.7_spmd.sunk.clone | while | flops 15728644 | bytes 258145 | solution.py:90
  132.6 3.9 %fusion.38 = f32[512]{0:T(512)S(1)} fusion(f32[4,512]{1,0:T(4,128)S(1)} %get-tuple-element.96, f32[4,512]{1,0:T(4,128)S(1)} %get-tuple-element.97, f32[512]{0:T(512)S(1)} %bitcast.118, f32[4,512]{1,0:T(4,128)S(1)} %get-tuple-element.99, f32[512]{0:T(512)S(1)} %bitcast.117, f32[4,512]{1,0:T(4,128)S(1)} %get-tuple-element.101, f32[512]{0:T(512)S(1)} %bitcast.116), kind=kLoop, calls=%fused_computation.10.clone.1.clone | loop fusion | flops 15728128 | bytes 40960 | tf_op jit(solution)/shard_map/while/body/eval_jaxpr/reduce_sum | solution.py:46
  136.7 3.9 %fusion.38 = f32[512]{0:T(512)S(1)} fusion(f32[4,512]{1,0:T(4,128)S(1)} %get-tuple-element.96, f32[4,512]{1,0:T(4,128)S(1)} %get-tuple-element.97, f32[512]{0:T(512)S(1)} %bitcast.118, f32[4,512]{1,0:T(4,128)S(1)} %get-tuple-element.99, f32[512]{0:T(512)S(1)} %bitcast.117, f32[4,512]{1,0:T(4,128)S(1)} %get-tuple-element.101, f32[512]{0:T(512)S(1)} %bitcast.116), kind=kLoop, calls=%fused_computation.10.clone.1.clone | loop fusion | flops 15728128 | bytes 40960 | tf_op jit(solution)/shard_map/while/body/eval_jaxpr/reduce_sum | solution.py:46
  140.8 3.9 %fusion.38 = f32[512]{0:T(512)S(1)} fusion(f32[4,512]{1,0:T(4,128)S(1)} %get-tuple-element.96, f32[4,512]{1,0:T(4,128)S(1)} %get-tuple-element.97, f32[512]{0:T(512)S(1)} %bitcast.118, f32[4,512]{1,0:T(4,128)S(1)} %get-tuple-element.99, f32[512]{0:T(512)S(1)} %bitcast.117, f32[4,512]{1,0:T(4,128)S(1)} %get-tuple-element.101, f32[512]{0:T(512)S(1)} %bitcast.116), kind=kLoop, calls=%fused_computation.10.clone.1.clone | loop fusion | flops 15728128 | bytes 40960 | tf_op jit(solution)/shard_map/while/body/eval_jaxpr/reduce_sum | solution.py:46
  144.8 3.9 %fusion.38 = f32[512]{0:T(512)S(1)} fusion(f32[4,512]{1,0:T(4,128)S(1)} %get-tuple-element.96, f32[4,512]{1,0:T(4,128)S(1)} %get-tuple-element.97, f32[512]{0:T(512)S(1)} %bitcast.118, f32[4,512]{1,0:T(4,128)S(1)} %get-tuple-element.99, f32[512]{0:T(512)S(1)} %bitcast.117, f32[4,512]{1,0:T(4,128)S(1)} %get-tuple-element.101, f32[512]{0:T(512)S(1)} %bitcast.116), kind=kLoop, calls=%fused_computation.10.clone.1.clone | loop fusion | flops 15728128 | bytes 40960 | tf_op jit(solution)/shard_map/while/body/eval_jaxpr/reduce_sum | solution.py:46
  148.9 3.9 %fusion.38 = f32[512]{0:T(512)S(1)} fusion(f32[4,512]{1,0:T(4,128)S(1)} %get-tuple-element.96, f32[4,512]{1,0:T(4,128)S(1)} %get-tuple-element.97, f32[512]{0:T(512)S(1)} %bitcast.118, f32[4,512]{1,0:T(4,128)S(1)} %get-tuple-element.99, f32[512]{0:T(512)S(1)} %bitcast.117, f32[4,512]{1,0:T(4,128)S(1)} %get-tuple-element.101, f32[512]{0:T(512)S(1)} %bitcast.116), kind=kLoop, calls=%fused_computation.10.clone.1.clone | loop fusion | flops 15728128 | bytes 40960 | tf_op jit(solution)/shard_map/while/body/eval_jaxpr/reduce_sum | solution.py:46
  153.0 3.9 %fusion.38 = f32[512]{0:T(512)S(1)} fusion(f32[4,512]{1,0:T(4,128)S(1)} %get-tuple-element.96, f32[4,512]{1,0:T(4,128)S(1)} %get-tuple-element.97, f32[512]{0:T(512)S(1)} %bitcast.118, f32[4,512]{1,0:T(4,128)S(1)} %get-tuple-element.99, f32[512]{0:T(512)S(1)} %bitcast.117, f32[4,512]{1,0:T(4,128)S(1)} %get-tuple-element.101, f32[512]{0:T(512)S(1)} %bitcast.116), kind=kLoop, calls=%fused_computation.10.clone.1.clone | loop fusion | flops 15728128 | bytes 40960 | tf_op jit(solution)/shard_map/while/body/eval_jaxpr/reduce_sum | solution.py:46
  157.1 3.9 %fusion.38 = f32[512]{0:T(512)S(1)} fusion(f32[4,512]{1,0:T(4,128)S(1)} %get-tuple-element.96, f32[4,512]{1,0:T(4,128)S(1)} %get-tuple-element.97, f32[512]{0:T(512)S(1)} %bitcast.118, f32[4,512]{1,0:T(4,128)S(1)} %get-tuple-element.99, f32[512]{0:T(512)S(1)} %bitcast.117, f32[4,512]{1,0:T(4,128)S(1)} %get-tuple-element.101, f32[512]{0:T(512)S(1)} %bitcast.116), kind=kLoop, calls=%fused_computation.10.clone.1.clone | loop fusion | flops 15728128 | bytes 40960 | tf_op jit(solution)/shard_map/while/body/eval_jaxpr/reduce_sum | solution.py:46
  161.2 3.9 %fusion.38 = f32[512]{0:T(512)S(1)} fusion(f32[4,512]{1,0:T(4,128)S(1)} %get-tuple-element.96, f32[4,512]{1,0:T(4,128)S(1)} %get-tuple-element.97, f32[512]{0:T(512)S(1)} %bitcast.118, f32[4,512]{1,0:T(4,128)S(1)} %get-tuple-element.99, f32[512]{0:T(512)S(1)} %bitcast.117, f32[4,512]{1,0:T(4,128)S(1)} %get-tuple-element.101, f32[512]{0:T(512)S(1)} %bitcast.116), kind=kLoop, calls=%fused_computation.10.clone.1.clone | loop fusion | flops 15728128 | bytes 40960 | tf_op jit(solution)/shard_map/while/body/eval_jaxpr/reduce_sum | solution.py:46
  165.3 4.0 %collective-permute-start.2 = (f32[128,128]{0,1:T(8,128)S(1)}, f32[128,128]{0,1:T(8,128)S(1)}, u32[]{:S(2)}, u32[]{:S(2)}) collective-permute-start(f32[128,128]{0,1:T(8,128)S(1)} %add.73), channel_id=1, source_target_pairs={{0,64},{16,80},{32,96},{48,112},{64,0},{80,16},{96,32},{112,48},{1... | collective-permute-start | bytes 196616 | tf_op jit(solution)/shard_map/ppermute | solution.py:15
  169.3 0.7 select_bitcast_fusion.4
  169.9 1.0 collective-permute-done.2
  171.0 11.7 %cholesky.109 = f32[128,128]{1,0:T(8,128)S(1)} custom-call(f32[128,128]{1,0:T(8,128)S(1)} %fusion.22), custom_call_target="Cholesky" | custom-call | tf_op jit(solution)/shard_map/jit(cholesky)/cholesky | solution.py:77
  183.3 5.8 %collective-permute-start.3 = (f32[128,128]{0,1:T(8,128)S(1)}, f32[128,128]{0,1:T(8,128)S(1)}, u32[]{:S(2)}, u32[]{:S(2)}) collective-permute-start(f32[128,128]{0,1:T(8,128)S(1)} %fusion.18), channel_id=1, source_target_pairs={{0,128},{16,144},{32,160},{48,176},{64,192},{80,208},{96,224},{112... | collective-permute-start | bytes 196616 | tf_op jit(solution)/shard_map/ppermute | solution.py:15
  189.2 3.0 %collective-permute-done.3 = f32[128,128]{0,1:T(8,128)S(1)} collective-permute-done((f32[128,128]{0,1:T(8,128)S(1)}, f32[128,128]{0,1:T(8,128)S(1)}, u32[]{:S(2)}, u32[]{:S(2)}) %collective-permute-start.3) | collective-permute-done | bytes 65568 | tf_op jit(solution)/shard_map/ppermute | solution.py:15
  192.2 8.8 %collective-permute-start.4 = (f32[128,128]{0,1:T(8,128)S(1)}, f32[128,128]{0,1:T(8,128)S(1)}, u32[]{:S(2)}, u32[]{:S(2)}) collective-permute-start(f32[128,128]{0,1:T(8,128)S(1)} %add.76), channel_id=1, source_target_pairs={{0,256},{16,272},{32,288},{48,304},{64,320},{80,336},{96,352},{112... | collective-permute-start | bytes 196616 | tf_op jit(solution)/shard_map/ppermute | solution.py:15
  201.6 1.5 collective-permute-done.4
  203.3 11.7 %cholesky.120 = f32[128,128]{1,0:T(8,128)S(1)} custom-call(f32[128,128]{1,0:T(8,128)S(1)} %fusion.17), custom_call_target="Cholesky" | custom-call | tf_op jit(solution)/shard_map/jit(cholesky)/cholesky | solution.py:82
  215.0 0.7 compare_reduce_fusion.1
  215.7 1.9 select_bitcast_fusion.1
  (108 shorter events, 5.9 us)
Async XLA Ops:
  0.6 4.3 %copy-start = (f32[1,8,128,128]{3,2,1,0:T(8,128)S(1)}, f32[1,8,128,128]{3,2,1,0:T(8,128)}, u32[]{:S(2)}) copy-start(f32[1,8,128,128]{3,2,1,0:T(8,128)} %param.14) | copy-start | bytes 1572868
  4.9 1.7 copy-start.1
  5.9 5.2 %copy-start.4 = (f32[1,8,512]{2,1,0:T(8,128)S(1)}, f32[1,8,512]{2,1,0:T(8,128)}, u32[]{:S(2)}) copy-start(f32[1,8,512]{2,1,0:T(8,128)} %param.18) | copy-start | bytes 49156
  5.9 5.2 %copy-start.5 = (s32[1,8]{1,0:T(1,128)S(1)}, s32[1,8]{1,0:T(1,128)}, u32[]{:S(2)}) copy-start(s32[1,8]{1,0:T(1,128)} %param.13) | copy-start | bytes 100
  5.9 5.3 %copy-start.3 = (f32[1,8,3,512]{3,1,2,0:T(8,128)S(1)}, f32[1,8,3,512]{3,1,2,0:T(8,128)}, u32[]{:S(2)}) copy-start(f32[1,8,3,512]{3,1,2,0:T(8,128)} %param.17) | copy-start | bytes 147460
  5.9 5.4 %copy-start.7 = (s32[1,4]{1,0:T(1,128)S(1)}, s32[1,4]{1,0:T(1,128)}, u32[]{:S(2)}) copy-start(s32[1,4]{1,0:T(1,128)} %param.19) | copy-start | bytes 52
  7.2 26.9 %copy-start.6 = (s32[1,8,4]{1,2,0:T(4,128)S(1)}, s32[1,8,4]{1,2,0:T(4,128)}, u32[]{:S(2)}) copy-start(s32[1,8,4]{1,2,0:T(4,128)} %param.20) | copy-start | bytes 388
  7.2 122.7 %collective-permute-start = (f32[128,128]{0,1:T(8,128)S(1)}, f32[128,128]{0,1:T(8,128)S(1)}, u32[]{:S(2)}, u32[]{:S(2)}) collective-permute-start(f32[128,128]{0,1:T(8,128)S(1)} %convolution_bitcast_fusion), channel_id=1, source_target_pairs={{0,16},{16,0},{32,48},{48,32},{64,80},{80,64},{96,112},{112,96},{1... | collective-permute-start | bytes 196616 | tf_op jit(solution)/shard_map/ppermute | solution.py:15
  12.0 117.2 %collective-permute-start.5 = (f32[1,2,4,512]{3,2,1,0:T(4,128)S(1)}, f32[1,2,4,512]{3,2,1,0:T(4,128)S(1)}, u32[]{:S(2)}, u32[]{:S(2)}) collective-permute-start(f32[1,2,4,512]{3,2,1,0:T(4,128)S(1)} %get-tuple-element.48), channel_id=1, source_target_pairs={{0,1},{1,2},{2,3},{3,4},{4,5},{5,6},{6,7},{7,8},{8,9},{9,10},{10,1... | collective-permute-start | bytes 49160 | tf_op jit(solution)/shard_map/ppermute | solution.py:26
  16.0 113.1 %collective-permute-start.6 = (f32[1,2,4,512]{3,2,1,0:T(4,128)S(1)}, f32[1,2,4,512]{3,2,1,0:T(4,128)S(1)}, u32[]{:S(2)}, u32[]{:S(2)}) collective-permute-start(f32[1,2,4,512]{3,2,1,0:T(4,128)S(1)} %get-tuple-element.49), channel_id=1, source_target_pairs={{1,0},{2,1},{3,2},{4,3},{5,4},{6,5},{7,6},{8,7},{9,8},{10,9},{11,1... | collective-permute-start | bytes 49160 | tf_op jit(solution)/shard_map/ppermute | solution.py:28
  130.0 35.2 %collective-permute-start.1 = (f32[128,128]{0,1:T(8,128)S(1)}, f32[128,128]{0,1:T(8,128)S(1)}, u32[]{:S(2)}, u32[]{:S(2)}) collective-permute-start(f32[128,128]{0,1:T(8,128)S(1)} %add.72), channel_id=1, source_target_pairs={{0,32},{16,48},{32,0},{48,16},{64,96},{80,112},{96,64},{112,80},{1... | collective-permute-start | bytes 196616 | tf_op jit(solution)/shard_map/ppermute | solution.py:15
  132.5 50.3 %copy-start.2 = (f32[1,4,128,128]{3,2,1,0:T(8,128)S(1)}, f32[1,4,128,128]{3,2,1,0:T(8,128)}, u32[]{:S(2)}) copy-start(f32[1,4,128,128]{3,2,1,0:T(8,128)} %param.16) | copy-start | bytes 786436
  165.3 5.6 %collective-permute-start.2 = (f32[128,128]{0,1:T(8,128)S(1)}, f32[128,128]{0,1:T(8,128)S(1)}, u32[]{:S(2)}, u32[]{:S(2)}) collective-permute-start(f32[128,128]{0,1:T(8,128)S(1)} %add.73), channel_id=1, source_target_pairs={{0,64},{16,80},{32,96},{48,112},{64,0},{80,16},{96,32},{112,48},{1... | collective-permute-start | bytes 196616 | tf_op jit(solution)/shard_map/ppermute | solution.py:15
  183.3 8.9 %collective-permute-start.3 = (f32[128,128]{0,1:T(8,128)S(1)}, f32[128,128]{0,1:T(8,128)S(1)}, u32[]{:S(2)}, u32[]{:S(2)}) collective-permute-start(f32[128,128]{0,1:T(8,128)S(1)} %fusion.18), channel_id=1, source_target_pairs={{0,128},{16,144},{32,160},{48,176},{64,192},{80,208},{96,224},{112... | collective-permute-start | bytes 196616 | tf_op jit(solution)/shard_map/ppermute | solution.py:15
  192.2 10.9 %collective-permute-start.4 = (f32[128,128]{0,1:T(8,128)S(1)}, f32[128,128]{0,1:T(8,128)S(1)}, u32[]{:S(2)}, u32[]{:S(2)}) collective-permute-start(f32[128,128]{0,1:T(8,128)S(1)} %add.76), channel_id=1, source_target_pairs={{0,256},{16,272},{32,288},{48,304},{64,320},{80,336},{96,352},{112... | collective-permute-start | bytes 196616 | tf_op jit(solution)/shard_map/ppermute | solution.py:15
where the time goes:
time: 220 us; the launch traced here: 218 us
  other arithmetic  169 us (77%)
  starting transfers between devices  33 us (15%)
  matrix products  6.23 us (3%)
  waiting for transfers between devices  5.49 us (2%)
  local copies, waits for them, and re-layouts  2.86 us (1%)
    another operation x4, other arithmetic, body(): leaf_factors = jnp.linalg.cholesky(grams)  94 us
    reduce_sum x8, other arithmetic, near_tile(): return coupling * jnp.sum(kernel * sources[None, :, 3, :], axis=(1, 2))  31.4 us
    ppermute x5, starting transfers between devices, from_partner(): lax.ppermute(value, axis, [(i, i ^ 1 << apart) for i in range(lax.axis_si...  25 us
    another operation x3, other arithmetic, body(): root_factor = jnp.linalg.cholesky(root_gram)  12.5 us
    another operation x3, other arithmetic, body(): node_factor = jnp.linalg.cholesky(node_gram)  12.4 us
    another operation x3, other arithmetic, body(): group_factor = jnp.linalg.cholesky(group_gram)  12.4 us
    ppermute x5, waiting for transfers between devices, from_partner(): lax.ppermute(value, axis, [(i, i ^ 1 << apart) for i in range(lax.axis_si...  5.49 us
  transfers between devices with their start and end apart: 7, of which 3 were waited for; matrix products, arithmetic and copies ran while one was open for 66% of the time, Pallas kernels for 0%

commit v1 on v0

v1 whole, which is shorter than its diff:
```python
import functools

import jax
import jax.numpy as jnp
from jax import lax
from jax.experimental import pallas as pl
from jax.experimental.pallas import tpu as pltpu
from jax.sharding import PartitionSpec as P

RANK = 128
PTS = 512
CHILDREN = 8
NB = 4
ROWS = 16
SPLIT = 48
MESH = pltpu.MESH if hasattr(pltpu, "MESH") else pl.DeviceIdType.MESH

f32 = jnp.float32
bf16 = jnp.bfloat16
highest = lax.Precision.HIGHEST
over_rows = (((0,), (0,)), ((), ()))


def split3(x):
    high = x.astype(bf16)
    rest = x - high.astype(f32)
    middle = rest.astype(bf16)
    return high, middle, (rest - middle.astype(f32)).astype(bf16)


def factor_panel(grams, uppers, mats, k, size):
    groups = size // 8
    sub = lax.broadcasted_iota(jnp.int32, (8, RANK), 0)
    lane = lax.broadcasted_iota(jnp.int32, (8, RANK), 1)
    start = pl.multiple_of(k * size, size)
    count = len(mats)

    def spread(x, s):
        return jnp.broadcast_to(x[s : s + 1, :], (8, RANK))

    rows = [[grams[m, pl.ds(pl.multiple_of(start + 8 * g, 8), 8), :] for g in range(groups)] for m in mats]
    columns = [
        [
            [
                jnp.take_along_axis(rows[i][g], jnp.full((8, RANK), start + j, jnp.int32), axis=1)
                if g >= j // 8
                else None
                for g in range(groups)
            ]
            for j in range(size)
        ]
        for i in range(count)
    ]
    upper = [[None] * groups for _ in mats]
    for r in range(size):
        gr, sr = divmod(r, 8)
        for i in range(count):
            pivot = spread(columns[i][r][gr], sr)
            inverse = 1.0 / pivot
            row = spread(rows[i][gr], sr)
            scaled = row * lax.rsqrt(pivot)
            upper[i][gr] = scaled if sr == 0 else jnp.where(sub >= sr, scaled, upper[i][gr])
            weights = {}
            for g in range(gr, groups):
                if g == gr and sr == 7:
                    continue
                weight = columns[i][r][g] * inverse
                weights[g] = jnp.where(sub > sr, weight, 0.0) if g == gr else weight
            for j in range(r + 1, size):
                entry = spread(columns[i][r][j // 8], j % 8)
                for g in range(max(gr, j // 8), groups):
                    if g in weights:
                        columns[i][j][g] = columns[i][j][g] - weights[g] * entry
            for g in weights:
                rows[i][g] = rows[i][g] - weights[g] * row
    for i, m in enumerate(mats):
        kept = [jnp.where(lane >= sub + (start + 8 * g), upper[i][g], 0.0) for g in range(groups)]
        panel = jnp.concatenate(kept, axis=0) if groups > 1 else kept[0]
        uppers[m, pl.ds(start, size), :] = panel
        high, middle, low = split3(panel)
        left = jnp.concatenate([high, high, high, middle, middle, low], axis=0)
        right = jnp.concatenate([high, middle, low, high, middle, high], axis=0)
        grams[m] = grams[m] - lax.dot_general(left, right, over_rows, preferred_element_type=f32)


def stacked(values):
    rows = lax.broadcasted_iota(jnp.int32, (8, PTS), 0)
    out = jnp.zeros((8, PTS), f32)
    for i, value in enumerate(values):
        out = jnp.where(rows == i, jnp.broadcast_to(value, (8, PTS)), out)
    return out


def source_features(x, y, z, q):
    x, y, z = x - 1.0, y - 1.0, z - 1.0
    flat, high2 = x * x + y * y, z * z
    one, none = jnp.ones_like(x), jnp.zeros_like(x)
    first = stacked([-2.0 * x, -2.0 * y, -2.0 * z, one, none, flat + high2 + 0.25])
    second = stacked([-2.0 * x * q, -2.0 * y * q, 4.0 * z * q, none, q, q * (flat - 2.0 * high2 + 0.25)])
    out = []
    for form in (first, second):
        high, middle, low = [piece.astype(f32) for piece in split3(form)]
        out += [high, middle, low, high, middle, high]
    return jnp.concatenate(out, axis=0)


def target_features(x, y, z):
    x, y, z = x - 1.0, y - 1.0, z - 1.0
    flat, high2 = x * x + y * y, z * z
    form = stacked([x, y, z, flat + high2, flat - 2.0 * high2, jnp.ones_like(x)])
    high, middle, low = [piece.astype(f32) for piece in split3(form)]
    return jnp.concatenate([high, high, high, middle, middle, low], axis=0).astype(bf16)


def field_of(targets, features, picks, width=256, depth=64):
    none = jnp.zeros((SPLIT, width), bf16)
    out = []
    for j in range(PTS // width):
        form = targets[:, j * width : (j + 1) * width]
        for_radius = jnp.concatenate([form, none], axis=0)
        for_weight = jnp.concatenate([none, form], axis=0)
        total = jnp.zeros((8, width), f32)
        for pick in picks:
            for c in range(PTS // depth):
                block = features[pick, c * depth : (c + 1) * depth, :]
                radius = jnp.dot(block, for_radius, preferred_element_type=f32)
                weight = jnp.dot(block, for_weight, preferred_element_type=f32)
                root = lax.rsqrt(radius)
                square = root * root
                value = (weight * root) * (square * square)
                total = total + jnp.sum(value.reshape(depth // 8, 8, width), axis=0)
        out.append(total)
    return jnp.concatenate(out, axis=1)


def kernel(
    slabs,
    spans,
    basis,
    leaf_transfer,
    node_transfer,
    group_transfer,
    positions,
    moments,
    counts,
    tiles,
    neighbours,
    leaf_out,
    node_out,
    group_out,
    root_out,
    near_out,
    own,
    faces,
    halo,
    features,
    grams,
    uppers,
    lifted,
    landed,
    summed,
    crossed,
    rooted,
    reduced,
    reduced_upper,
    face_send,
    face_recv,
    one_send,
    one_recv,
    two_send,
    two_recv,
    cross_send,
    cross_recv,
    three_send,
    three_recv,
):
    leaf = lax.axis_index("leaf")
    slab = lax.axis_index("slab")
    member, group = leaf % CHILDREN, leaf // CHILDREN
    peers = [group * CHILDREN + (member + d) % CHILDREN for d in range(1, CHILDREN)]
    kin = [((group + d) % spans) * CHILDREN + member for d in range(1, spans)]
    above, below = (slab + 1) % slabs, (slab + slabs - 1) % slabs
    barrier = pltpu.get_barrier_semaphore()
    for other in peers + kin:
        pl.semaphore_signal(barrier, inc=1, device_id={"leaf": other}, device_id_type=MESH)
    for other in (above, below):
        pl.semaphore_signal(barrier, inc=1, device_id={"slab": other}, device_id_type=MESH)

    points = lax.broadcasted_iota(jnp.int32, (1, PTS), 1)
    for l in range(CHILDREN):
        for axis in range(3):
            own[l, axis : axis + 1, :] = positions[axis, l : l + 1, :]
        own[l, 3:4, :] = moments[l : l + 1, :] * (points < counts[0, l]).astype(f32)
    for f in range(4):
        faces[f] = own[tiles[0, f]]

    slots = lax.broadcasted_iota(jnp.int32, (PTS, RANK), 0)
    inner = []
    for l in range(CHILDREN):
        live = jnp.where(slots < counts[0, l], basis[l].astype(f32), 0.0).astype(bf16)
        gram = lax.dot_general(live, live, over_rows, preferred_element_type=f32)
        grams[l] = gram
        inner.append(jnp.dot(gram, leaf_transfer[l], precision=highest, preferred_element_type=f32))
    every = leaf_transfer[...].reshape(CHILDREN * RANK, RANK)
    node = lax.dot_general(every, jnp.concatenate(inner, axis=0), over_rows, precision=highest, preferred_element_type=f32)
    grams[CHILDREN] = node

    def congruent(transfer, gram):
        product = jnp.dot(gram, transfer, precision=highest, preferred_element_type=f32)
        return lax.dot_general(transfer, product, over_rows, precision=highest, preferred_element_type=f32)

    to_group = congruent(node_transfer[...], node)
    to_root = congruent(group_transfer[group], to_group)
    for c in range(CHILDREN):
        lifted[c, 0] = to_group[c * ROWS : (c + 1) * ROWS, :]
        lifted[c, 1] = to_root[c * ROWS : (c + 1) * ROWS, :]

    pl.semaphore_wait(barrier, len(peers) + len(kin) + 2)

    def remote(source, target, send, recv, where):
        return pltpu.make_async_remote_copy(
            src_ref=source, dst_ref=target, send_sem=send, recv_sem=recv, device_id=where, device_id_type=MESH
        )

    up = remote(faces.at[pl.ds(2, 2)], halo.at[pl.ds(0, 2)], face_send.at[0], face_recv.at[0], {"slab": above})
    down = remote(faces.at[pl.ds(0, 2)], halo.at[pl.ds(2, 2)], face_send.at[1], face_recv.at[1], {"slab": below})
    firsts = [
        remote(
            lifted.at[(member + d) % CHILDREN],
            landed.at[d - 1],
            one_send.at[d - 1],
            one_recv.at[d - 1],
            {"leaf": peers[d - 1]},
        )
        for d in range(1, CHILDREN)
    ]
    for copy in firsts:
        copy.start()
    up.start()
    down.start()

    def own_features(l, carry):
        s = own[l]
        features[l] = source_features(s[0:1], s[1:2], s[2:3], s[3:4]).T.astype(bf16)
        return carry

    lax.fori_loop(0, CHILDREN, own_features, 0)

    def first_panels(k, carry):
        factor_panel(grams, uppers, range(CHILDREN + 1), k, 8)
        return carry

    def second_panels(k, carry):
        factor_panel(reduced, reduced_upper, range(2), k, 16)
        return carry

    def near(l, carry):
        s = own[l]
        total = field_of(
            target_features(s[0:1], s[1:2], s[2:3]), features, [neighbours[k, l] for k in range(NB)]
        )
        near_out[pl.ds(l, 1), :] = jnp.where(
            points < counts[0, l], 0.03 * jnp.sum(total, axis=0, keepdims=True), 0.0
        )
        return carry

    lax.fori_loop(0, RANK // 8, first_panels, 0)

    for copy in firsts:
        copy.wait()
    total = lifted[member]
    for d in range(1, CHILDREN):
        total = total + landed[d - 1]
    summed[...] = total
    mine = pl.ds(pl.multiple_of(member * ROWS, ROWS), ROWS)
    reduced[0, mine, :] = total[0]
    seconds = [
        remote(
            summed.at[0], reduced.at[0, mine], two_send.at[d - 1], two_recv.at[d - 1], {"leaf": peers[d - 1]}
        )
        for d in range(1, CHILDREN)
    ]
    crosses = [
        remote(summed.at[1], crossed.at[d - 1], cross_send.at[d - 1], cross_recv.at[d - 1], {"leaf": kin[d - 1]})
        for d in range(1, spans)
    ]
    for copy in crosses + seconds:
        copy.start()

    up.wait()
    down.wait()

    def halo_features(e, carry):
        s = halo[e]
        there = jnp.where(e < 2, slab > 0, slab < slabs - 1).astype(f32)
        features[CHILDREN + e] = source_features(s[0:1], s[1:2], s[2:3], s[3:4] * there).T.astype(bf16)
        return carry

    lax.fori_loop(0, 4, halo_features, 0)
    lax.fori_loop(0, 3, near, 0)

    for copy in crosses:
        copy.wait()
    total = summed[1]
    for d in range(1, spans):
        total = total + crossed[d - 1]
    rooted[...] = total
    reduced[1, mine, :] = total
    thirds = [
        remote(rooted, reduced.at[1, mine], three_send.at[d - 1], three_recv.at[d - 1], {"leaf": peers[d - 1]})
        for d in range(1, CHILDREN)
    ]
    for copy in thirds:
        copy.start()
    lax.fori_loop(3, CHILDREN, near, 0)
    for copy in seconds + thirds:
        copy.wait()
    lax.fori_loop(0, RANK // 16, second_panels, 0)
    for l in range(CHILDREN):
        leaf_out[l] = uppers[l].T
    node_out[...] = uppers[CHILDREN].T
    group_out[...] = reduced_upper[0].T
    root_out[...] = reduced_upper[1].T


def body(
    leaf_basis,
    point_counts,
    leaf_transfer,
    node_transfer,
    group_transfer,
    positions,
    moments,
    send_tiles,
    neighbours,
):
    spans = lax.axis_size("leaf") // CHILDREN
    slabs = lax.axis_size("slab")
    vmem = pl.BlockSpec(memory_space=pltpu.VMEM)
    smem = pl.BlockSpec(memory_space=pltpu.SMEM)
    square = jax.ShapeDtypeStruct((RANK, RANK), f32)
    dma = pltpu.SemaphoreType.DMA
    leaf, node, group, root, near = pl.pallas_call(
        functools.partial(kernel, slabs, spans),
        out_shape=(
            jax.ShapeDtypeStruct((CHILDREN, RANK, RANK), f32),
            square,
            square,
            square,
            jax.ShapeDtypeStruct((CHILDREN, PTS), f32),
        ),
        in_specs=[vmem] * 6 + [smem] * 3,
        out_specs=(vmem,) * 5,
        scratch_shapes=[
            pltpu.VMEM((CHILDREN, 4, PTS), f32),
            pltpu.VMEM((4, 4, PTS), f32),
            pltpu.VMEM((4, 4, PTS), f32),
            pltpu.VMEM((CHILDREN + 4, PTS, 2 * SPLIT), bf16),
            pltpu.VMEM((CHILDREN + 1, RANK, RANK), f32),
            pltpu.VMEM((CHILDREN + 1, RANK, RANK), f32),
            pltpu.VMEM((CHILDREN, 2, ROWS, RANK), f32),
            pltpu.VMEM((CHILDREN - 1, 2, ROWS, RANK), f32),
            pltpu.VMEM((2, ROWS, RANK), f32),
            pltpu.VMEM((spans - 1, ROWS, RANK), f32),
            pltpu.VMEM((ROWS, RANK), f32),
            pltpu.VMEM((2, RANK, RANK), f32),
            pltpu.VMEM((2, RANK, RANK), f32),
            dma((2,)),
            dma((2,)),
            dma((CHILDREN - 1,)),
            dma((CHILDREN - 1,)),
            dma((CHILDREN - 1,)),
            dma((CHILDREN - 1,)),
            dma((spans - 1,)),
            dma((spans - 1,)),
            dma((CHILDREN - 1,)),
            dma((CHILDREN - 1,)),
        ],
        compiler_params=pltpu.CompilerParams(collective_id=0, has_side_effects=True),
        name="upsweep",
    )(
        leaf_basis[0],
        leaf_transfer[0],
        node_transfer[0, 0],
        group_transfer[0],
        jnp.transpose(positions[0], (1, 0, 2)),
        moments[0],
        point_counts,
        send_tiles,
        jnp.transpose(neighbours[0]),
    )
    return leaf[None], node[None, None], group[None, None], root[None, None], near[None]


def solution(mesh):
    in_specs = (
        P("slab", "leaf", None, None),
        P("slab", "leaf"),
        P("slab", "leaf", None, None),
        P("slab", "leaf", None, None),
        P("slab", None, None, None),
        P("slab", "leaf", None, None),
        P("slab", "leaf", None),
        P("slab", "leaf"),
        P("slab", "leaf", None),
    )
    out_specs = (
        P("slab", "leaf", None, None),
        P("slab", "leaf", None, None),
        P("slab", "leaf", None, None),
        P("slab", "leaf", None, None),
        P("slab", "leaf", None),
    )
    return jax.shard_map(body, mesh=mesh, in_specs=in_specs, out_specs=out_specs, check_vma=False)
```

time: 220 us -> 43.7 us (0.20)
  other arithmetic: 169 us -> 0 us
  Pallas kernels: 0 us -> 37.4 us
  starting transfers between devices: 33 us -> 0 us
  matrix products: 6.23 us -> 0 us
  waiting for transfers between devices: 5.49 us -> 0 us
    another operation x13 -> x0, other arithmetic: 131 us -> none  [the longest x4 94 us: body(): leaf_factors = jnp.linalg.cholesky(grams)]
    pallas_call x0 -> x1, Pallas kernels: none -> 37.4 us  [body(): pl.pallas_call(functools.partial(kernel, slabs, spans), out_shape=(jax.Sh...]
    ppermute x7 -> x0, starting transfers between devices: 33 us -> none  [the longest x5 25 us: from_partner(): lax.ppermute(value, axis, [(i, i ^ 1 << apart) for i in range(lax.axis_si...]
    reduce_sum x8 -> x0, other arithmetic: 31.4 us -> none  [near_tile(): return coupling * jnp.sum(kernel * sources[None, :, 3, :], axis=(1, 2))]
    dot_general x7 -> x0, matrix products: 6.23 us -> none  [the longest x1 3.44 us: body(): lax.dot_general(masked, masked, (((1,), (1,)), ((0,), (0,))), preferred_e...]
    ppermute x7 -> x0, waiting for transfers between devices: 5.49 us -> none  [the longest x5 5.49 us: from_partner(): lax.ppermute(value, axis, [(i, i ^ 1 << apart) for i in range(lax.axis_si...]
    unnamed x17 -> x13, local copies, waits for them, and re-layouts: 0.09 us -> 4.95 us
    broadcast_in_dim x5 -> x0, other arithmetic: 4.79 us -> none  [the longest x1 1.91 us: body(): root_factor[None, None]]
  transfers between devices with their start and end apart: 7 -> 0, of which waited for: 3 -> 0; matrix products, arithmetic and copies ran while one was open for 66% -> 0% of each run, Pallas kernels for 0% -> 0%
where the time goes in v1:
time: 43.7 us; the launch traced here: 43 us
  Pallas kernels  37.4 us (86%)
  local copies, waits for them, and re-layouts  4.95 us (11%)
  between operations  0.66 us (2%)
    pallas_call x1, Pallas kernels, body(): pl.pallas_call(functools.partial(kernel, slabs, spans), out_shape=(jax.Sh...  37.4 us
    unnamed x13, local copies, waits for them, and re-layouts  4.95 us

profile of v1, /device:TPU:1, one launch (start us, length us, event | category | flops | bytes accessed | tf_op | source)
XLA Modules:
  0.0 43.0 jit_solution(13327437231746118857)
XLA Ops:
  0.6 37.4 %upsweep.1 = (f32[8,128,128]{2,1,0:T(8,128)}, f32[128,128]{1,0:T(8,128)}, f32[128,128]{1,0:T(8,128)}, f32[128,128]{1,0:T(8,128)}, f32[8,512]{1,0:T(8,128)}) custom-call(bf16[8,512,128]{2,1,0:T(8,128)(2,1)} %bitcast.16, f32[8,128,128]{2,1,0:T(8,128)} %bitcast.18, f32[128,128]{1,0:T(8,128)} %bitcast.20, f32[4,128,128]{2,1,0:T(8,128)} %bitcast.19, ...), custom_call_target="tpu_custom_call" | custom-call | tf_op jit(solution)/shard_map/upsweep/pallas_call | solution.py:343
  38.1 0.0 copy-start.2
  38.1 1.9 %copy.19 = f32[1,8,128,128]{3,2,1,0:T(8,128)} copy(f32[1,8,128,128]{3,2,1,0:T(8,128)} %bitcast.17) | data formatting | bytes 1048576
  40.0 0.0 copy-done.2
  40.0 0.0 copy-start.1
  40.0 0.6 %copy.20 = f32[1,1,128,128]{3,2,1,0:T(8,128)} copy(f32[1,1,128,128]{3,2,1,0:T(8,128)S(1)} %bitcast.23) | data formatting | bytes 131072
  40.6 0.2 copy-done.1
  40.9 0.0 copy-start
  40.9 0.6 %copy.21 = f32[1,1,128,128]{3,2,1,0:T(8,128)} copy(f32[1,1,128,128]{3,2,1,0:T(8,128)S(1)} %bitcast.22) | data formatting | bytes 131072
  41.5 0.2 copy-done
  41.7 0.0 copy-start.3
  41.7 0.6 %copy.22 = f32[1,1,128,128]{3,2,1,0:T(8,128)} copy(f32[1,1,128,128]{3,2,1,0:T(8,128)S(1)} %bitcast.21) | data formatting | bytes 131072
  42.4 0.1 copy-done.3
  42.4 0.6 %copy.23 = f32[1,8,512]{2,1,0:T(8,128)} copy(f32[1,8,512]{2,1,0:T(8,128)S(1)} %bitcast.26) | data formatting | bytes 32768
Async XLA Ops:
  38.1 1.9 %copy-start.2 = (f32[128,128]{1,0:T(8,128)S(1)}, f32[128,128]{1,0:T(8,128)}, u32[]{:S(2)}) copy-start(f32[128,128]{1,0:T(8,128)} %get-tuple-element.11) | copy-start | bytes 196612
  40.0 0.9 %copy-start.1 = (f32[128,128]{1,0:T(8,128)S(1)}, f32[128,128]{1,0:T(8,128)}, u32[]{:S(2)}) copy-start(f32[128,128]{1,0:T(8,128)} %get-tuple-element.12) | copy-start | bytes 196612
  40.9 0.9 %copy-start = (f32[128,128]{1,0:T(8,128)S(1)}, f32[128,128]{1,0:T(8,128)}, u32[]{:S(2)}) copy-start(f32[128,128]{1,0:T(8,128)} %get-tuple-element.13) | copy-start | bytes 196612
  41.7 0.7 %copy-start.3 = (f32[8,512]{1,0:T(8,128)S(1)}, f32[8,512]{1,0:T(8,128)}, u32[]{:S(2)}) copy-start(f32[8,512]{1,0:T(8,128)} %get-tuple-element.14) | copy-start | bytes 49156

commit v2 on v1

--- a/solution.py
+++ b/solution.py
@@ -12,6 +12,7 @@
 CHILDREN = 8
 NB = 4
 ROWS = 16
+EARLY = 3
 SPLIT = 48
 MESH = pltpu.MESH if hasattr(pltpu, "MESH") else pl.DeviceIdType.MESH
 
@@ -135,7 +136,7 @@
 
 def kernel(
     slabs,
-    spans,
+    nodes,
     basis,
     leaf_transfer,
     node_transfer,
@@ -145,43 +146,41 @@
     counts,
     tiles,
     neighbours,
-    leaf_out,
-    node_out,
-    group_out,
-    root_out,
-    near_out,
+    uppers,
+    reduced,
+    partial,
+    features,
     own,
     faces,
     halo,
-    features,
     grams,
-    uppers,
     lifted,
     landed,
     summed,
-    crossed,
+    rising,
+    risen,
     rooted,
-    reduced,
-    reduced_upper,
+    gathered,
+    joined,
     face_send,
     face_recv,
     one_send,
     one_recv,
     two_send,
     two_recv,
-    cross_send,
-    cross_recv,
-    three_send,
-    three_recv,
+    rise_send,
+    rise_recv,
+    root_send,
+    root_recv,
 ):
     leaf = lax.axis_index("leaf")
     slab = lax.axis_index("slab")
     member, group = leaf % CHILDREN, leaf // CHILDREN
     peers = [group * CHILDREN + (member + d) % CHILDREN for d in range(1, CHILDREN)]
-    kin = [((group + d) % spans) * CHILDREN + member for d in range(1, spans)]
+    others = [(leaf + d) % nodes for d in range(1, nodes)]
     above, below = (slab + 1) % slabs, (slab + slabs - 1) % slabs
     barrier = pltpu.get_barrier_semaphore()
-    for other in peers + kin:
+    for other in others:
         pl.semaphore_signal(barrier, inc=1, device_id={"leaf": other}, device_id_type=MESH)
     for other in (above, below):
         pl.semaphore_signal(barrier, inc=1, device_id={"slab": other}, device_id_type=MESH)
@@ -211,11 +210,13 @@
 
     to_group = congruent(node_transfer[...], node)
     to_root = congruent(group_transfer[group], to_group)
+    part = RANK // nodes
     for c in range(CHILDREN):
-        lifted[c, 0] = to_group[c * ROWS : (c + 1) * ROWS, :]
-        lifted[c, 1] = to_root[c * ROWS : (c + 1) * ROWS, :]
-
-    pl.semaphore_wait(barrier, len(peers) + len(kin) + 2)
+        lifted[c] = to_group[c * ROWS : (c + 1) * ROWS, :]
+    for c in range(nodes):
+        rising[c] = to_root[c * part : (c + 1) * part, :]
+
+    pl.semaphore_wait(barrier, len(others) + 2)
 
     def remote(source, target, send, recv, where):
         return pltpu.make_async_remote_copy(
@@ -224,6 +225,8 @@
 
     up = remote(faces.at[pl.ds(2, 2)], halo.at[pl.ds(0, 2)], face_send.at[0], face_recv.at[0], {"slab": above})
     down = remote(faces.at[pl.ds(0, 2)], halo.at[pl.ds(2, 2)], face_send.at[1], face_recv.at[1], {"slab": below})
+    up.start()
+    down.start()
     firsts = [
         remote(
             lifted.at[(member + d) % CHILDREN],
@@ -233,11 +236,18 @@
             {"leaf": peers[d - 1]},
         )
         for d in range(1, CHILDREN)
+    ] + [
+        remote(
+            rising.at[(leaf + d) % nodes],
+            risen.at[d - 1],
+            rise_send.at[d - 1],
+            rise_recv.at[d - 1],
+            {"leaf": others[d - 1]},
+        )
+        for d in range(1, nodes)
     ]
     for copy in firsts:
         copy.start()
-    up.start()
-    down.start()
 
     def own_features(l, carry):
         s = own[l]
@@ -246,25 +256,18 @@
 
     lax.fori_loop(0, CHILDREN, own_features, 0)
 
-    def first_panels(k, carry):
+    def panels(k, carry):
         factor_panel(grams, uppers, range(CHILDREN + 1), k, 8)
         return carry
 
-    def second_panels(k, carry):
-        factor_panel(reduced, reduced_upper, range(2), k, 16)
-        return carry
-
     def near(l, carry):
         s = own[l]
-        total = field_of(
-            target_features(s[0:1], s[1:2], s[2:3]), features, [neighbours[k, l] for k in range(NB)]
-        )
-        near_out[pl.ds(l, 1), :] = jnp.where(
-            points < counts[0, l], 0.03 * jnp.sum(total, axis=0, keepdims=True), 0.0
+        partial[l] = field_of(
+            target_features(s[0:1], s[1:2], s[2:3]), features, [neighbours[k, l] for k in range(EARLY)]
         )
         return carry
 
-    lax.fori_loop(0, RANK // 8, first_panels, 0)
+    lax.fori_loop(0, RANK // 8, panels, 0)
 
     for copy in firsts:
         copy.wait()
@@ -273,20 +276,21 @@
         total = total + landed[d - 1]
     summed[...] = total
     mine = pl.ds(pl.multiple_of(member * ROWS, ROWS), ROWS)
-    reduced[0, mine, :] = total[0]
+    joined[mine, :] = total
+    total = rising[leaf]
+    for d in range(1, nodes):
+        total = total + risen[d - 1]
+    rooted[...] = total
+    gathered[leaf] = total
     seconds = [
-        remote(
-            summed.at[0], reduced.at[0, mine], two_send.at[d - 1], two_recv.at[d - 1], {"leaf": peers[d - 1]}
-        )
+        remote(summed, joined.at[mine], two_send.at[d - 1], two_recv.at[d - 1], {"leaf": peers[d - 1]})
         for d in range(1, CHILDREN)
+    ] + [
+        remote(rooted, gathered.at[leaf], root_send.at[d - 1], root_recv.at[d - 1], {"leaf": others[d - 1]})
+        for d in range(1, nodes)
     ]
-    crosses = [
-        remote(summed.at[1], crossed.at[d - 1], cross_send.at[d - 1], cross_recv.at[d - 1], {"leaf": kin[d - 1]})
-        for d in range(1, spans)
-    ]
-    for copy in crosses + seconds:
+    for copy in seconds:
         copy.start()
-
     up.wait()
     down.wait()
 
@@ -297,30 +301,40 @@
         return carry
 
     lax.fori_loop(0, 4, halo_features, 0)
-    lax.fori_loop(0, 3, near, 0)
-
-    for copy in crosses:
+    lax.fori_loop(0, CHILDREN, near, 0)
+    for copy in seconds:
         copy.wait()
-    total = summed[1]
-    for d in range(1, spans):
-        total = total + crossed[d - 1]
-    rooted[...] = total
-    reduced[1, mine, :] = total
-    thirds = [
-        remote(rooted, reduced.at[1, mine], three_send.at[d - 1], three_recv.at[d - 1], {"leaf": peers[d - 1]})
-        for d in range(1, CHILDREN)
-    ]
-    for copy in thirds:
-        copy.start()
-    lax.fori_loop(3, CHILDREN, near, 0)
-    for copy in seconds + thirds:
-        copy.wait()
-    lax.fori_loop(0, RANK // 16, second_panels, 0)
+    reduced[0] = joined[...]
+    for c in range(nodes):
+        reduced[1, c * part : (c + 1) * part, :] = gathered[c]
+
+
+def finish(
+    uppers, reduced, partial, features, positions, counts, neighbours,
+    leaf_out, node_out, group_out, root_out, near_out, leaves, grams, tops, done,
+):
+    points = lax.broadcasted_iota(jnp.int32, (1, PTS), 1)
     for l in range(CHILDREN):
-        leaf_out[l] = uppers[l].T
+        leaves[l] = uppers[l].T
+    copy = pltpu.make_async_copy(leaves, leaf_out, done)
+    copy.start()
     node_out[...] = uppers[CHILDREN].T
-    group_out[...] = reduced_upper[0].T
-    root_out[...] = reduced_upper[1].T
+    grams[...] = reduced[...]
+
+    def step(l, carry):
+        row = pl.ds(l, 1)
+        total = partial[l]
+        if EARLY < NB:
+            form = target_features(positions[0, row, :], positions[1, row, :], positions[2, row, :])
+            total = total + field_of(form, features, [neighbours[k, l] for k in range(EARLY, NB)])
+        factor_panel(grams, tops, range(2), l, 16)
+        near_out[row, :] = jnp.where(points < counts[0, l], 0.03 * jnp.sum(total, axis=0, keepdims=True), 0.0)
+        return carry
+
+    lax.fori_loop(0, CHILDREN, step, 0)
+    group_out[...] = tops[0].T
+    root_out[...] = tops[1].T
+    copy.wait()
 
 
 def body(
@@ -334,14 +348,66 @@
     send_tiles,
     neighbours,
 ):
-    spans = lax.axis_size("leaf") // CHILDREN
+    nodes = lax.axis_size("leaf")
     slabs = lax.axis_size("slab")
     vmem = pl.BlockSpec(memory_space=pltpu.VMEM)
     smem = pl.BlockSpec(memory_space=pltpu.SMEM)
     square = jax.ShapeDtypeStruct((RANK, RANK), f32)
     dma = pltpu.SemaphoreType.DMA
+    part = RANK // nodes
+    places = jnp.transpose(positions[0], (1, 0, 2))
+    links = jnp.transpose(neighbours[0])
+    uppers, reduced, partial, features = pl.pallas_call(
+        functools.partial(kernel, slabs, nodes),
+        out_shape=(
+            jax.ShapeDtypeStruct((CHILDREN + 1, RANK, RANK), f32),
+            jax.ShapeDtypeStruct((2, RANK, RANK), f32),
+            jax.ShapeDtypeStruct((CHILDREN, 8, PTS), f32),
+            jax.ShapeDtypeStruct((CHILDREN + 4, PTS, 2 * SPLIT), bf16),
+        ),
+        in_specs=[vmem] * 6 + [smem] * 3,
+        out_specs=(vmem,) * 4,
+        scratch_shapes=[
+            pltpu.VMEM((CHILDREN, 4, PTS), f32),
+            pltpu.VMEM((4, 4, PTS), f32),
+            pltpu.VMEM((4, 4, PTS), f32),
+            pltpu.VMEM((CHILDREN + 1, RANK, RANK), f32),
+            pltpu.VMEM((CHILDREN, ROWS, RANK), f32),
+            pltpu.VMEM((CHILDREN - 1, ROWS, RANK), f32),
+            pltpu.VMEM((ROWS, RANK), f32),
+            pltpu.VMEM((nodes, part, RANK), f32),
+            pltpu.VMEM((nodes - 1, part, RANK), f32),
+            pltpu.VMEM((part, RANK), f32),
+            pltpu.VMEM((nodes, part, RANK), f32),
+            pltpu.VMEM((RANK, RANK), f32),
+            dma((2,)),
+            dma((2,)),
+            dma((CHILDREN - 1,)),
+            dma((CHILDREN - 1,)),
+            dma((CHILDREN - 1,)),
+            dma((CHILDREN - 1,)),
+            dma((nodes - 1,)),
+            dma((nodes - 1,)),
+            dma((nodes - 1,)),
+            dma((nodes - 1,)),
+        ],
+        compiler_params=pltpu.CompilerParams(
+            collective_id=0, has_side_effects=True, vmem_limit_bytes=24 * 1024 * 1024
+        ),
+        name="upsweep",
+    )(
+        leaf_basis[0],
+        leaf_transfer[0],
+        node_transfer[0, 0],
+        group_transfer[0],
+        places,
+        moments[0],
+        point_counts,
+        send_tiles,
+        links,
+    )
     leaf, node, group, root, near = pl.pallas_call(
-        functools.partial(kernel, slabs, spans),
+        finish,
         out_shape=(
             jax.ShapeDtypeStruct((CHILDREN, RANK, RANK), f32),
             square,
@@ -349,46 +415,17 @@
             square,
             jax.ShapeDtypeStruct((CHILDREN, PTS), f32),
         ),
-        in_specs=[vmem] * 6 + [smem] * 3,
-        out_specs=(vmem,) * 5,
+        in_specs=[vmem] * 5 + [smem] * 2,
+        out_specs=(pl.BlockSpec(memory_space=pl.ANY),) + (vmem,) * 4,
         scratch_shapes=[
-            pltpu.VMEM((CHILDREN, 4, PTS), f32),
-            pltpu.VMEM((4, 4, PTS), f32),
-            pltpu.VMEM((4, 4, PTS), f32),
-            pltpu.VMEM((CHILDREN + 4, PTS, 2 * SPLIT), bf16),
-            pltpu.VMEM((CHILDREN + 1, RANK, RANK), f32),
-            pltpu.VMEM((CHILDREN + 1, RANK, RANK), f32),
-            pltpu.VMEM((CHILDREN, 2, ROWS, RANK), f32),
-            pltpu.VMEM((CHILDREN - 1, 2, ROWS, RANK), f32),
-            pltpu.VMEM((2, ROWS, RANK), f32),
-            pltpu.VMEM((spans - 1, ROWS, RANK), f32),
-            pltpu.VMEM((ROWS, RANK), f32),
+            pltpu.VMEM((CHILDREN, RANK, RANK), f32),
             pltpu.VMEM((2, RANK, RANK), f32),
             pltpu.VMEM((2, RANK, RANK), f32),
-            dma((2,)),
-            dma((2,)),
-            dma((CHILDREN - 1,)),
-            dma((CHILDREN - 1,)),
-            dma((CHILDREN - 1,)),
-            dma((CHILDREN - 1,)),
-            dma((spans - 1,)),
-            dma((spans - 1,)),
-            dma((CHILDREN - 1,)),
-            dma((CHILDREN - 1,)),
+            dma,
         ],
-        compiler_params=pltpu.CompilerParams(collective_id=0, has_side_effects=True),
-        name="upsweep",
-    )(
-        leaf_basis[0],
-        leaf_transfer[0],
-        node_transfer[0, 0],
-        group_transfer[0],
-        jnp.transpose(positions[0], (1, 0, 2)),
-        moments[0],
-        point_counts,
-        send_tiles,
-        jnp.transpose(neighbours[0]),
-    )
+        compiler_params=pltpu.CompilerParams(vmem_limit_bytes=24 * 1024 * 1024),
+        name="finish",
+    )(uppers, reduced, partial, features, places, point_counts, links)
     return leaf[None], node[None, None], group[None, None], root[None, None], near[None]
 
 

time: 43.7 us -> 48.2 us (1.10)
  local copies, waits for them, and re-layouts: 4.95 us -> 7.55 us
  Pallas kernels: 37.4 us -> 39.5 us
    unnamed x13 -> x18, local copies, waits for them, and re-layouts: 4.95 us -> 7.55 us
    pallas_call x1 -> x2, Pallas kernels: 37.4 us -> 39.5 us  [the longest x1 33.1 us: body(): pl.pallas_call(functools.partial(kernel, slabs, nodes), out_shape=(jax.Sh...]
where the time goes in v2:
time: 48.2 us; the launch traced here: 47.7 us
  Pallas kernels  39.5 us (82%)
  local copies, waits for them, and re-layouts  7.55 us (16%)
  between operations  0.66 us (1%)
    pallas_call x1, Pallas kernels, body(): pl.pallas_call(functools.partial(kernel, slabs, nodes), out_shape=(jax.Sh...  33.1 us
    unnamed x18, local copies, waits for them, and re-layouts  7.55 us
    pallas_call x1, Pallas kernels, body(): pl.pallas_call(finish, out_shape=(jax.ShapeDtypeStruct((CHILDREN, RANK, R...  6.46 us

profile of v2, /device:TPU:1, one launch (start us, length us, event | category | flops | bytes accessed | tf_op | source)
XLA Modules:
  0.0 47.7 jit_solution(3975138845043441177)
XLA Ops:
  0.6 0.0 copy-start
  0.6 1.2 %copy-done = bf16[1,8,512,128]{3,2,1,0:T(8,128)(2,1)S(1)} copy-done((bf16[1,8,512,128]{3,2,1,0:T(8,128)(2,1)S(1)}, bf16[1,8,512,128]{3,2,1,0:T(8,128)(2,1)}, u32[]{:S(2)}) %copy-start) | copy-done | bytes 1048600
  1.9 0.0 copy-start.1
  1.9 1.0 %copy-done.1 = f32[1,8,128,128]{3,2,1,0:T(8,128)S(1)} copy-done((f32[1,8,128,128]{3,2,1,0:T(8,128)S(1)}, f32[1,8,128,128]{3,2,1,0:T(8,128)}, u32[]{:S(2)}) %copy-start.1) | copy-done | bytes 524312
  2.9 0.0 copy-start.2
  2.9 0.9 %copy-done.2 = f32[1,4,128,128]{3,2,1,0:T(8,128)S(1)} copy-done((f32[1,4,128,128]{3,2,1,0:T(8,128)S(1)}, f32[1,4,128,128]{3,2,1,0:T(8,128)}, u32[]{:S(2)}) %copy-start.2) | copy-done | bytes 262168
  3.9 0.0 copy-start.3
  3.9 0.8 %copy-done.3 = f32[1,8,3,512]{3,1,2,0:T(8,128)S(1)} copy-done((f32[1,8,3,512]{3,1,2,0:T(8,128)S(1)}, f32[1,8,3,512]{3,1,2,0:T(8,128)}, u32[]{:S(2)}) %copy-start.3) | copy-done | bytes 49176
  4.7 0.0 copy-start.4
  4.7 0.8 %copy-done.4 = f32[1,1,128,128]{3,2,1,0:T(8,128)S(1)} copy-done((f32[1,1,128,128]{3,2,1,0:T(8,128)S(1)}, f32[1,1,128,128]{3,2,1,0:T(8,128)}, u32[]{:S(2)}) %copy-start.4) | copy-done | bytes 65560
  5.5 0.0 copy-start.5
  5.5 0.7 %copy-done.5 = f32[1,8,512]{2,1,0:T(8,128)S(1)} copy-done((f32[1,8,512]{2,1,0:T(8,128)S(1)}, f32[1,8,512]{2,1,0:T(8,128)}, u32[]{:S(2)}) %copy-start.5) | copy-done | bytes 16408
  6.2 0.0 copy-start.6
  6.2 0.7 %copy-done.6 = s32[1,8,4]{1,2,0:T(4,128)S(1)} copy-done((s32[1,8,4]{1,2,0:T(4,128)S(1)}, s32[1,8,4]{1,2,0:T(4,128)}, u32[]{:S(2)}) %copy-start.6) | copy-done | bytes 152
  6.9 0.0 copy-start.7
  6.9 0.7 %copy-done.7 = s32[1,8]{1,0:T(1,128)S(1)} copy-done((s32[1,8]{1,0:T(1,128)S(1)}, s32[1,8]{1,0:T(1,128)}, u32[]{:S(2)}) %copy-start.7) | copy-done | bytes 56
  7.5 0.0 copy-start.8
  7.5 0.7 %copy-done.8 = s32[1,4]{1,0:T(1,128)S(1)} copy-done((s32[1,4]{1,0:T(1,128)S(1)}, s32[1,4]{1,0:T(1,128)}, u32[]{:S(2)}) %copy-start.8) | copy-done | bytes 40
  8.2 33.1 %upsweep.1 = (f32[9,128,128]{2,1,0:T(8,128)S(1)}, f32[2,128,128]{2,1,0:T(8,128)S(1)}, f32[8,8,512]{2,1,0:T(8,128)S(1)}, bf16[12,512,96]{2,1,0:T(8,128)(2,1)S(1)}) custom-call(bf16[8,512,128]{2,1,0:T(8,128)(2,1)S(1)} %bitcast.16, f32[8,128,128]{2,1,0:T(8,128)S(1)} %bitcast.17, f32[128,128]{1,0:T(8,128)S(1)} %bitcast.21, f32[4,128,128]{2,1,0:T(8,128)S(1)} %bitcast.18, ...), custom_call_target="tpu_custom_call" | custom-call | tf_op jit(solution)/shard_map/upsweep/pallas_call | solution.py:360
  41.3 6.5 %finish.1 = (f32[8,128,128]{2,1,0:T(8,128)}, f32[128,128]{1,0:T(8,128)}, f32[128,128]{1,0:T(8,128)}, f32[128,128]{1,0:T(8,128)}, f32[8,512]{1,0:T(8,128)}) custom-call(f32[9,128,128]{2,1,0:T(8,128)S(1)} %get-tuple-element.14.uppers, f32[2,128,128]{2,1,0:T(8,128)S(1)} %get-tuple-element.15.reduced, f32[8,8,512]{2,1,0:T(8,128)S(1)} %get-tuple-element.16.partial, ...), custom_call_target="tpu_custom_call" | custom-call | tf_op jit(solution)/shard_map/finish/pallas_call | solution.py:409
Async XLA Ops:
  0.6 1.2 %copy-start = (bf16[1,8,512,128]{3,2,1,0:T(8,128)(2,1)S(1)}, bf16[1,8,512,128]{3,2,1,0:T(8,128)(2,1)}, u32[]{:S(2)}) copy-start(bf16[1,8,512,128]{3,2,1,0:T(8,128)(2,1)} %param.9) | copy-start | bytes 3145732
  1.9 1.0 %copy-start.1 = (f32[1,8,128,128]{3,2,1,0:T(8,128)S(1)}, f32[1,8,128,128]{3,2,1,0:T(8,128)}, u32[]{:S(2)}) copy-start(f32[1,8,128,128]{3,2,1,0:T(8,128)} %param.11) | copy-start | bytes 1572868
  2.9 0.9 %copy-start.2 = (f32[1,4,128,128]{3,2,1,0:T(8,128)S(1)}, f32[1,4,128,128]{3,2,1,0:T(8,128)}, u32[]{:S(2)}) copy-start(f32[1,4,128,128]{3,2,1,0:T(8,128)} %param.13) | copy-start | bytes 786436
  3.9 0.8 %copy-start.3 = (f32[1,8,3,512]{3,1,2,0:T(8,128)S(1)}, f32[1,8,3,512]{3,1,2,0:T(8,128)}, u32[]{:S(2)}) copy-start(f32[1,8,3,512]{3,1,2,0:T(8,128)} %param.14) | copy-start | bytes 147460
  4.7 0.8 %copy-start.4 = (f32[1,1,128,128]{3,2,1,0:T(8,128)S(1)}, f32[1,1,128,128]{3,2,1,0:T(8,128)}, u32[]{:S(2)}) copy-start(f32[1,1,128,128]{3,2,1,0:T(8,128)} %param.12) | copy-start | bytes 196612
  5.5 0.7 %copy-start.5 = (f32[1,8,512]{2,1,0:T(8,128)S(1)}, f32[1,8,512]{2,1,0:T(8,128)}, u32[]{:S(2)}) copy-start(f32[1,8,512]{2,1,0:T(8,128)} %param.15) | copy-start | bytes 49156
  6.2 0.7 %copy-start.6 = (s32[1,8,4]{1,2,0:T(4,128)S(1)}, s32[1,8,4]{1,2,0:T(4,128)}, u32[]{:S(2)}) copy-start(s32[1,8,4]{1,2,0:T(4,128)} %param.17) | copy-start | bytes 388
  6.9 0.7 %copy-start.7 = (s32[1,8]{1,0:T(1,128)S(1)}, s32[1,8]{1,0:T(1,128)}, u32[]{:S(2)}) copy-start(s32[1,8]{1,0:T(1,128)} %counts.3) | copy-start | bytes 100
  7.5 0.7 %copy-start.8 = (s32[1,4]{1,0:T(1,128)S(1)}, s32[1,4]{1,0:T(1,128)}, u32[]{:S(2)}) copy-start(s32[1,4]{1,0:T(1,128)} %tiles.1) | copy-start | bytes 52

commit v3 on v2

--- a/solution.py
+++ b/solution.py
@@ -12,6 +12,7 @@
 CHILDREN = 8
 NB = 4
 ROWS = 16
+AHEAD = 2
 EARLY = 3
 SPLIT = 48
 MESH = pltpu.MESH if hasattr(pltpu, "MESH") else pl.DeviceIdType.MESH
@@ -137,6 +138,19 @@
 def kernel(
     slabs,
     nodes,
+    basis_hbm,
+    leaf_transfer_hbm,
+    node_transfer_hbm,
+    group_transfer_hbm,
+    positions_hbm,
+    moments_hbm,
+    counts_hbm,
+    tiles_hbm,
+    neighbours_hbm,
+    uppers,
+    reduced,
+    partial,
+    features,
     basis,
     leaf_transfer,
     node_transfer,
@@ -146,10 +160,8 @@
     counts,
     tiles,
     neighbours,
-    uppers,
-    reduced,
-    partial,
-    features,
+    basis_done,
+    loaded,
     own,
     faces,
     halo,
@@ -179,6 +191,24 @@
     peers = [group * CHILDREN + (member + d) % CHILDREN for d in range(1, CHILDREN)]
     others = [(leaf + d) % nodes for d in range(1, nodes)]
     above, below = (slab + 1) % slabs, (slab + slabs - 1) % slabs
+    loads = [
+        pltpu.make_async_copy(source, target, loaded.at[i])
+        for i, (source, target) in enumerate(
+            [
+                (counts_hbm, counts),
+                (tiles_hbm, tiles),
+                (positions_hbm, positions),
+                (moments_hbm, moments),
+                (neighbours_hbm, neighbours),
+                (leaf_transfer_hbm, leaf_transfer),
+                (node_transfer_hbm, node_transfer),
+                (group_transfer_hbm.at[group], group_transfer),
+            ]
+        )
+    ]
+    blocks = [pltpu.make_async_copy(basis_hbm.at[l], basis.at[l], basis_done.at[l]) for l in range(CHILDREN)]
+    for copy in loads[:4] + blocks + loads[4:]:
+        copy.start()
     barrier = pltpu.get_barrier_semaphore()
     for other in others:
         pl.semaphore_signal(barrier, inc=1, device_id={"leaf": other}, device_id_type=MESH)
@@ -186,6 +216,8 @@
         pl.semaphore_signal(barrier, inc=1, device_id={"slab": other}, device_id_type=MESH)
 
     points = lax.broadcasted_iota(jnp.int32, (1, PTS), 1)
+    for copy in loads[:4]:
+        copy.wait()
     for l in range(CHILDREN):
         for axis in range(3):
             own[l, axis : axis + 1, :] = positions[axis, l : l + 1, :]
@@ -195,6 +227,8 @@
 
     slots = lax.broadcasted_iota(jnp.int32, (PTS, RANK), 0)
     inner = []
+    for copy in blocks + loads[4:]:
+        copy.wait()
     for l in range(CHILDREN):
         live = jnp.where(slots < counts[0, l], basis[l].astype(f32), 0.0).astype(bf16)
         gram = lax.dot_general(live, live, over_rows, preferred_element_type=f32)
@@ -209,12 +243,32 @@
         return lax.dot_general(transfer, product, over_rows, precision=highest, preferred_element_type=f32)
 
     to_group = congruent(node_transfer[...], node)
-    to_root = congruent(group_transfer[group], to_group)
+    to_root = congruent(group_transfer[...], to_group)
     part = RANK // nodes
     for c in range(CHILDREN):
         lifted[c] = to_group[c * ROWS : (c + 1) * ROWS, :]
     for c in range(nodes):
         rising[c] = to_root[c * part : (c + 1) * part, :]
+
+    def own_features(l, carry):
+        s = own[l]
+        features[l] = source_features(s[0:1], s[1:2], s[2:3], s[3:4]).T.astype(bf16)
+        return carry
+
+    lax.fori_loop(0, CHILDREN, own_features, 0)
+
+    def panels(k, carry):
+        factor_panel(grams, uppers, range(CHILDREN + 1), k, 8)
+        return carry
+
+    def near(l, carry):
+        s = own[l]
+        partial[l] = field_of(
+            target_features(s[0:1], s[1:2], s[2:3]), features, [neighbours[k, l] for k in range(EARLY)]
+        )
+        return carry
+
+    lax.fori_loop(0, AHEAD, panels, 0)
 
     pl.semaphore_wait(barrier, len(others) + 2)
 
@@ -249,25 +303,7 @@
     for copy in firsts:
         copy.start()
 
-    def own_features(l, carry):
-        s = own[l]
-        features[l] = source_features(s[0:1], s[1:2], s[2:3], s[3:4]).T.astype(bf16)
-        return carry
-
-    lax.fori_loop(0, CHILDREN, own_features, 0)
-
-    def panels(k, carry):
-        factor_panel(grams, uppers, range(CHILDREN + 1), k, 8)
-        return carry
-
-    def near(l, carry):
-        s = own[l]
-        partial[l] = field_of(
-            target_features(s[0:1], s[1:2], s[2:3]), features, [neighbours[k, l] for k in range(EARLY)]
-        )
-        return carry
-
-    lax.fori_loop(0, RANK // 8, panels, 0)
+    lax.fori_loop(AHEAD, RANK // 8, panels, 0)
 
     for copy in firsts:
         copy.wait()
@@ -310,9 +346,34 @@
 
 
 def finish(
-    uppers, reduced, partial, features, positions, counts, neighbours,
-    leaf_out, node_out, group_out, root_out, near_out, leaves, grams, tops, done,
+    uppers,
+    reduced,
+    partial,
+    features,
+    positions_hbm,
+    counts_hbm,
+    neighbours_hbm,
+    leaf_out,
+    node_out,
+    group_out,
+    root_out,
+    near_out,
+    positions,
+    counts,
+    neighbours,
+    loaded,
+    leaves,
+    grams,
+    tops,
+    done,
 ):
+    loads = [
+        pltpu.make_async_copy(positions_hbm, positions, loaded.at[0]),
+        pltpu.make_async_copy(counts_hbm, counts, loaded.at[1]),
+        pltpu.make_async_copy(neighbours_hbm, neighbours, loaded.at[2]),
+    ]
+    for copy in loads:
+        copy.start()
     points = lax.broadcasted_iota(jnp.int32, (1, PTS), 1)
     for l in range(CHILDREN):
         leaves[l] = uppers[l].T
@@ -320,6 +381,8 @@
     copy.start()
     node_out[...] = uppers[CHILDREN].T
     grams[...] = reduced[...]
+    for load in loads:
+        load.wait()
 
     def step(l, carry):
         row = pl.ds(l, 1)
@@ -335,6 +398,10 @@
     group_out[...] = tops[0].T
     root_out[...] = tops[1].T
     copy.wait()
+
+
+def pin(array):
+    return pltpu.with_memory_space_constraint(array, pltpu.HBM)
 
 
 def body(
@@ -351,7 +418,7 @@
     nodes = lax.axis_size("leaf")
     slabs = lax.axis_size("slab")
     vmem = pl.BlockSpec(memory_space=pltpu.VMEM)
-    smem = pl.BlockSpec(memory_space=pltpu.SMEM)
+    hbm = pl.BlockSpec(memory_space=pltpu.HBM)
     square = jax.ShapeDtypeStruct((RANK, RANK), f32)
     dma = pltpu.SemaphoreType.DMA
     part = RANK // nodes
@@ -365,9 +432,20 @@
             jax.ShapeDtypeStruct((CHILDREN, 8, PTS), f32),
             jax.ShapeDtypeStruct((CHILDREN + 4, PTS, 2 * SPLIT), bf16),
         ),
-        in_specs=[vmem] * 6 + [smem] * 3,
+        in_specs=[hbm] * 9,
         out_specs=(vmem,) * 4,
         scratch_shapes=[
+            pltpu.VMEM((CHILDREN, PTS, RANK), bf16),
+            pltpu.VMEM((CHILDREN, RANK, RANK), f32),
+            pltpu.VMEM((RANK, RANK), f32),
+            pltpu.VMEM((RANK, RANK), f32),
+            pltpu.VMEM((3, CHILDREN, PTS), f32),
+            pltpu.VMEM((CHILDREN, PTS), f32),
+            pltpu.SMEM((1, CHILDREN), jnp.int32),
+            pltpu.SMEM((1, 4), jnp.int32),
+            pltpu.SMEM((NB, CHILDREN), jnp.int32),
+            dma((CHILDREN,)),
+            dma((8,)),
             pltpu.VMEM((CHILDREN, 4, PTS), f32),
             pltpu.VMEM((4, 4, PTS), f32),
             pltpu.VMEM((4, 4, PTS), f32),
@@ -396,15 +474,15 @@
         ),
         name="upsweep",
     )(
-        leaf_basis[0],
-        leaf_transfer[0],
-        node_transfer[0, 0],
-        group_transfer[0],
-        places,
-        moments[0],
-        point_counts,
-        send_tiles,
-        links,
+        pin(leaf_basis[0]),
+        pin(leaf_transfer[0]),
+        pin(node_transfer[0, 0]),
+        pin(group_transfer[0]),
+        pin(places),
+        pin(moments[0]),
+        pin(point_counts),
+        pin(send_tiles),
+        pin(links),
     )
     leaf, node, group, root, near = pl.pallas_call(
         finish,
@@ -415,9 +493,13 @@
             square,
             jax.ShapeDtypeStruct((CHILDREN, PTS), f32),
         ),
-        in_specs=[vmem] * 5 + [smem] * 2,
-        out_specs=(pl.BlockSpec(memory_space=pl.ANY),) + (vmem,) * 4,
+        in_specs=[vmem] * 4 + [hbm] * 3,
+        out_specs=(hbm,) + (vmem,) * 4,
         scratch_shapes=[
+            pltpu.VMEM((3, CHILDREN, PTS), f32),
+            pltpu.SMEM((1, CHILDREN), jnp.int32),
+            pltpu.SMEM((NB, CHILDREN), jnp.int32),
+            dma((3,)),
             pltpu.VMEM((CHILDREN, RANK, RANK), f32),
             pltpu.VMEM((2, RANK, RANK), f32),
             pltpu.VMEM((2, RANK, RANK), f32),
@@ -425,7 +507,7 @@
         ],
         compiler_params=pltpu.CompilerParams(vmem_limit_bytes=24 * 1024 * 1024),
         name="finish",
-    )(uppers, reduced, partial, features, places, point_counts, links)
+    )(uppers, reduced, partial, features, pin(places), pin(point_counts), pin(links))
     return leaf[None], node[None, None], group[None, None], root[None, None], near[None]
 
 

time: 48.2 us -> 38.8 us (0.80)
  local copies, waits for them, and re-layouts: 7.55 us -> 0 us
  Pallas kernels: 39.5 us -> 38 us
    unnamed x18 -> x0, local copies, waits for them, and re-layouts: 7.55 us -> none
    pallas_call x1, Pallas kernels: 33.1 us -> 31.5 us  [body(): pl.pallas_call(functools.partial(kernel, slabs, nodes), out_shape=(jax.Sh...]
where the time goes in v3:
time: 38.8 us; the launch traced here: 38.6 us
  Pallas kernels  38 us (98%)
  between operations  0.64 us (2%)
    pallas_call x1, Pallas kernels, body(): pl.pallas_call(functools.partial(kernel, slabs, nodes), out_shape=(jax.Sh...  31.5 us
    pallas_call x1, Pallas kernels, body(): pl.pallas_call(finish, out_shape=(jax.ShapeDtypeStruct((CHILDREN, RANK, R...  6.52 us

profile of v3, /device:TPU:1, one launch (start us, length us, event | category | flops | bytes accessed | tf_op | source)
XLA Modules:
  0.0 38.6 jit_solution(4845494467672404145)
XLA Ops:
  0.6 31.5 %upsweep.1 = (f32[9,128,128]{2,1,0:T(8,128)S(1)}, f32[2,128,128]{2,1,0:T(8,128)S(1)}, f32[8,8,512]{2,1,0:T(8,128)S(1)}, bf16[12,512,96]{2,1,0:T(8,128)(2,1)S(1)}) custom-call(bf16[8,512,128]{2,1,0:T(8,128)(2,1)} %bitcast.16, f32[8,128,128]{2,1,0:T(8,128)} %bitcast.17, f32[128,128]{1,0:T(8,128)} %bitcast.21, f32[4,128,128]{2,1,0:T(8,128)} %bitcast.18, ...), custom_call_target="tpu_custom_call" | custom-call | tf_op jit(solution)/shard_map/upsweep/pallas_call | solution.py:427
  32.1 6.5 %finish.1 = (f32[8,128,128]{2,1,0:T(8,128)}, f32[128,128]{1,0:T(8,128)}, f32[128,128]{1,0:T(8,128)}, f32[128,128]{1,0:T(8,128)}, f32[8,512]{1,0:T(8,128)}) custom-call(f32[9,128,128]{2,1,0:T(8,128)S(1)} %get-tuple-element.14.uppers, f32[2,128,128]{2,1,0:T(8,128)S(1)} %get-tuple-element.15.reduced, f32[8,8,512]{2,1,0:T(8,128)S(1)} %get-tuple-element.16.partial, ...), custom_call_target="tpu_custom_call" | custom-call | tf_op jit(solution)/shard_map/finish/pallas_call | solution.py:487

commit v4 on v3

--- a/solution.py
+++ b/solution.py
@@ -12,7 +12,8 @@
 CHILDREN = 8
 NB = 4
 ROWS = 16
-AHEAD = 2
+BEFORE = 1
+AHEAD = 4
 EARLY = 3
 SPLIT = 48
 MESH = pltpu.MESH if hasattr(pltpu, "MESH") else pl.DeviceIdType.MESH
@@ -234,16 +235,21 @@
         gram = lax.dot_general(live, live, over_rows, preferred_element_type=f32)
         grams[l] = gram
         inner.append(jnp.dot(gram, leaf_transfer[l], precision=highest, preferred_element_type=f32))
+    to_parent = node_transfer[...]
+    to_top = jnp.dot(to_parent, group_transfer[...], precision=highest, preferred_element_type=f32)
     every = leaf_transfer[...].reshape(CHILDREN * RANK, RANK)
     node = lax.dot_general(every, jnp.concatenate(inner, axis=0), over_rows, precision=highest, preferred_element_type=f32)
     grams[CHILDREN] = node
 
-    def congruent(transfer, gram):
-        product = jnp.dot(gram, transfer, precision=highest, preferred_element_type=f32)
-        return lax.dot_general(transfer, product, over_rows, precision=highest, preferred_element_type=f32)
-
-    to_group = congruent(node_transfer[...], node)
-    to_root = congruent(group_transfer[...], to_group)
+    def product(left, right):
+        return jnp.dot(left, right, precision=highest, preferred_element_type=f32)
+
+    def from_left(transfer, right):
+        return lax.dot_general(transfer, right, over_rows, precision=highest, preferred_element_type=f32)
+
+    both = product(node, jnp.concatenate([to_parent, to_top], axis=1))
+    to_group = from_left(to_parent, both[:, :RANK])
+    to_root = from_left(to_top, both[:, RANK:])
     part = RANK // nodes
     for c in range(CHILDREN):
         lifted[c] = to_group[c * ROWS : (c + 1) * ROWS, :]
@@ -305,6 +311,18 @@
 
     lax.fori_loop(AHEAD, RANK // 8, panels, 0)
 
+    up.wait()
+    down.wait()
+
+    def halo_features(e, carry):
+        s = halo[e]
+        there = jnp.where(e < 2, slab > 0, slab < slabs - 1).astype(f32)
+        features[CHILDREN + e] = source_features(s[0:1], s[1:2], s[2:3], s[3:4] * there).T.astype(bf16)
+        return carry
+
+    lax.fori_loop(0, 4, halo_features, 0)
+    lax.fori_loop(0, BEFORE, near, 0)
+
     for copy in firsts:
         copy.wait()
     total = lifted[member]
@@ -327,17 +345,7 @@
     ]
     for copy in seconds:
         copy.start()
-    up.wait()
-    down.wait()
-
-    def halo_features(e, carry):
-        s = halo[e]
-        there = jnp.where(e < 2, slab > 0, slab < slabs - 1).astype(f32)
-        features[CHILDREN + e] = source_features(s[0:1], s[1:2], s[2:3], s[3:4] * there).T.astype(bf16)
-        return carry
-
-    lax.fori_loop(0, 4, halo_features, 0)
-    lax.fori_loop(0, CHILDREN, near, 0)
+    lax.fori_loop(BEFORE, CHILDREN, near, 0)
     for copy in seconds:
         copy.wait()
     reduced[0] = joined[...]

time: 38.8 us -> 38.9 us (level)
  no operation moved by 1% of the time
where the time goes in v4:
time: 38.9 us; the launch traced here: 38.6 us
  Pallas kernels  38 us (98%)
  between operations  0.64 us (2%)
    pallas_call x1, Pallas kernels, body(): pl.pallas_call(functools.partial(kernel, slabs, nodes), out_shape=(jax.Sh...  31.5 us
    pallas_call x1, Pallas kernels, body(): pl.pallas_call(finish, out_shape=(jax.ShapeDtypeStruct((CHILDREN, RANK, R...  6.51 us

profile of v4, /device:TPU:1, one launch (start us, length us, event | category | flops | bytes accessed | tf_op | source)
XLA Modules:
  0.0 38.6 jit_solution(17536009383865910780)
XLA Ops:
  0.6 31.5 %upsweep.1 = (f32[9,128,128]{2,1,0:T(8,128)S(1)}, f32[2,128,128]{2,1,0:T(8,128)S(1)}, f32[8,8,512]{2,1,0:T(8,128)S(1)}, bf16[12,512,96]{2,1,0:T(8,128)(2,1)S(1)}) custom-call(bf16[8,512,128]{2,1,0:T(8,128)(2,1)} %bitcast.16, f32[8,128,128]{2,1,0:T(8,128)} %bitcast.17, f32[128,128]{1,0:T(8,128)} %bitcast.21, f32[4,128,128]{2,1,0:T(8,128)} %bitcast.18, ...), custom_call_target="tpu_custom_call" | custom-call | tf_op jit(solution)/shard_map/upsweep/pallas_call | solution.py:435
  32.1 6.5 %finish.1 = (f32[8,128,128]{2,1,0:T(8,128)}, f32[128,128]{1,0:T(8,128)}, f32[128,128]{1,0:T(8,128)}, f32[128,128]{1,0:T(8,128)}, f32[8,512]{1,0:T(8,128)}) custom-call(f32[9,128,128]{2,1,0:T(8,128)S(1)} %get-tuple-element.14.uppers, f32[2,128,128]{2,1,0:T(8,128)S(1)} %get-tuple-element.15.reduced, f32[8,8,512]{2,1,0:T(8,128)S(1)} %get-tuple-element.16.partial, ...), custom_call_target="tpu_custom_call" | custom-call | tf_op jit(solution)/shard_map/finish/pallas_call | solution.py:495
